TPU v7x, 256 devices: a whole 4x4x8 slice. The times are simulated.
256 devices in a mesh: rows: 64 (over z, y, core), grp: 4 (over x).
Axes of the slice: x: 4, y: 4, z: 8, core: 2. Of those that a mesh axis runs over, the one named last changes fastest.
Arguments:
- matrix: float32 [524288, 512], P(('rows', 'grp')), may hold values from -6 to 6
- sign_bits: int32 [524288], P(('rows', 'grp')), may hold values from 0 to 1
- samples: int32 [16, 16384], P('grp'), may hold values from 0 to 32767, as said below
Outputs:
- r_factor: float32 [512, 512], replicated
- solved: float32 [524288, 512], P(('rows', 'grp'))
Inputs may be any that keep to these rules, and one draw needn't show every extreme that they name: `samples`: each row names 16384 distinct positions of a batch, exactly one of each pair 2 k and 2 k + 1, in any order.
All inputs are finite; a program needn't handle non-finite values.
Results may differ from a plain program's by a relative error of at most 0.0001.
Values sent between devices are 32-bit elements; how exact they have to be, the bound alone decides.
No kernel may reach another device: no remote copies, remote signals or barrier semaphores. Data moves between devices by JAX's collectives and lax.ppermute only.
A program may use at most 128 MiB of HBM per device.

v0:
```python
import jax
import jax.numpy as jnp
from jax import lax
from jax.sharding import PartitionSpec as P

INNER = 256


def cosine_sorted(size):
    evens = jnp.arange(0, size, 2, dtype=jnp.int32)
    odds = jnp.arange(1, size, 2, dtype=jnp.int32)
    freq = jnp.concatenate([evens, odds])[:, None]
    place = jnp.arange(size, dtype=jnp.int32)[None, :]
    phase = (2 * place + 1) * freq % (4 * size)
    weight = jnp.where(freq == 0, 1.0, 2.0).astype(jnp.float32) / size
    return jnp.sqrt(weight) * jnp.cos(jnp.pi * phase.astype(jnp.float32) / (2 * size))


def cosine(size):
    freq = jnp.arange(size, dtype=jnp.int32)[:, None]
    place = jnp.arange(size, dtype=jnp.int32)[None, :]
    phase = (2 * place + 1) * freq % (4 * size)
    weight = jnp.where(freq == 0, 1.0, 2.0).astype(jnp.float32) / size
    return jnp.sqrt(weight) * jnp.cos(jnp.pi * phase.astype(jnp.float32) / (2 * size))


def pair_parity(chosen):
    return jnp.zeros(chosen.shape, jnp.int32).at[chosen // 2].set(chosen % 2)


def local(matrix, sign_bits, samples):
    nrows = lax.axis_size("rows")
    ngroups = lax.axis_size("grp")
    batches, half = samples.shape
    per_device = matrix.shape[0] // batches
    width = matrix.shape[1]
    narrow = width // nrows
    total = per_device * nrows
    outer = total // INNER
    halfin = INNER // 2
    signed = matrix * (1 - 2 * sign_bits).astype(jnp.float32)[:, None]
    local_rows = signed.reshape(batches, per_device // INNER, INNER, width)
    c_inner = cosine_sorted(INNER)
    c_outer = cosine(outer)
    first = jnp.einsum("qp,bspn->bnsq", c_inner, local_rows, precision=lax.Precision.HIGHEST)
    first = first.reshape(batches, width, per_device)
    owned = lax.all_to_all(first, "rows", split_axis=1, concat_axis=2, tiled=True)
    mixed = jnp.einsum(
        "ap,bcpq->bcaq",
        c_outer,
        owned.reshape(batches, narrow, outer, INNER),
        precision=lax.Precision.HIGHEST,
    )
    parity = jax.vmap(pair_parity)(samples)
    even_rows = mixed[:, :, :, :halfin].reshape(batches, narrow, half)
    odd_rows = mixed[:, :, :, halfin:].reshape(batches, narrow, half)
    picked = jnp.where(parity[:, None, :] == 1, odd_rows, even_rows)
    rows_back = lax.all_to_all(picked, "rows", split_axis=2, concat_axis=1, tiled=True)
    gram = jnp.einsum("bnr,bmr->nm", rows_back, rows_back, precision=lax.Precision.HIGHEST)
    gram = lax.psum(gram, ("rows", "grp"))
    gram = gram / (ngroups * batches * half)
    lower = jnp.linalg.cholesky(gram)
    inverse = jax.scipy.linalg.solve_triangular(
        lower, jnp.eye(width, dtype=jnp.float32), lower=True
    )
    solved = jnp.dot(
        matrix, inverse.T, precision=lax.Precision.HIGHEST, preferred_element_type=jnp.float32
    )
    return (lower.T, solved)


def solution(mesh):
    placed = (P(("rows", "grp"), None), P(("rows", "grp")), P("grp", None))
    return jax.shard_map(
        local,
        mesh=mesh,
        in_specs=placed,
        out_specs=(P(), P(("rows", "grp"), None)),
        check_vma=False,
    )
```

profile of v0, /device:TPU:2, one launch (start us, length us, event | category | flops | bytes accessed | tf_op | source)
XLA Modules:
  0.0 941.8 jit_solution(5274258557876319001)
XLA Ops:
  7.9 2.5 broadcast_multiply_fusion
  10.5 7.6 fusion.30
  18.0 5.4 copy.18
  23.5 12.5 %all-to-all-start = ((f32[4,512,512]{2,0,1:T(4,128)}), f32[4,512,512]{2,0,1:T(4,128)}, u32[]{:S(2)}, u32[]{:S(2)}) async-start(f32[4,512,512]{2,0,1:T(4,128)} %copy.18), calls=%async_computation | async-start | bytes 8388608 | tf_op jit(solution)/shard_map/all_to_all | solution.py:47
  37.3 239.6 %scatter_custom_fusion = s32[65536]{0:T(1024)S(1)} fusion(s32[65536]{0:T(1024)S(1)} %bitcast.107, s32[65536]{0:T(1024)S(1)} %bitcast.108, s32[]{:T(128)} %copy.55), kind=kCustom, calls=%fused_computation.83 | custom fusion | bytes 262148
  277.0 3.5 copy.38
  280.6 4.4 copy.20
  285.0 5.2 reshape.110
  290.2 8.8 convolution_bitcast_fusion.1
  310.8 20.2 %copy.24 = f32[4,8,16384]{1,0,2:T(4,128)} copy(f32[4,8,16384]{2,1,0:T(8,128)S(1)} %broadcast_select_fusion) | data formatting | bytes 4194304 | tf_op jit(solution)/shard_map/jit(_where)/select_n | solution.py:57
  330.9 41.0 %reshape.149 = f32[64,1,8192]{2,1,0:T(1,128)S(1)} reshape(f32[16384,4,8]{2,1,0:T(4,128)} %bitcast.102) | data formatting | bytes 4194304
  371.9 62.0 %all_to_all.33 = f32[64,1,8192]{2,1,0:T(1,128)} all-to-all(f32[64,1,8192]{2,1,0:T(1,128)S(1)} %reshape.149), channel_id=1, replica_groups=mesh['rows'=64,'grp'=4] {'rows'}, dimensions={0} | all-to-all | bytes 4194304 | tf_op jit(solution)/shard_map/all_to_all | solution.py:58
  434.4 7.5 reduce.28
  442.0 41.6 %reshape.150 = f32[16384,4,8]{2,1,0:T(4,128)} reshape(f32[64,8192]{1,0:T(8,128)S(1)} %reduce.28) | data formatting | bytes 4194304
  483.6 23.7 %copy.25 = f32[4,8,64,256]{3,1,2,0:T(8,128)S(1)} copy(f32[4,8,64,256]{1,0,3,2:T(4,128)} %bitcast.103) | data formatting | bytes 4194304 | tf_op jit(solution)/shard_map/all_to_all | solution.py:58
  507.3 4.5 fusion.2
  513.0 254.1 %all-reduce.3.cloned.1.call-done = f32[512,512]{0,1:T(8,128)} async-done(((f32[512,512]{0,1:T(8,128)}), f32[512,512]{0,1:T(8,128)}) %all-reduce.3.cloned.1.call-update) | async-done | bytes 1048592 | tf_op jit(solution)/shard_map/psum | solution.py:60
  770.0 11.7 %cholesky.104 = f32[128,128]{1,0:T(8,128)S(1)} custom-call(f32[128,128]{1,0:T(8,128)S(1)} %cholesky.266), custom_call_target="Cholesky" | custom-call | tf_op jit(solution)/shard_map/jit(cholesky)/cholesky | solution.py:62
  781.8 9.8 %custom-call.31 = f32[1,128,128]{1,2,0:T(8,128)S(1)} custom-call(f32[1,128,128]{2,1,0:T(8,128)S(1)} %get-tuple-element.41), custom_call_target="InvertDiagBlocksLowerTriangular" | custom-call | tf_op jit(solution)/shard_map/jit(cholesky)/cholesky | solution.py:62
  794.4 11.9 %cholesky.217 = f32[128,128]{1,0:T(8,128)S(1)} custom-call(f32[128,128]{1,0:T(8,128)S(1)} %cholesky.270), custom_call_target="Cholesky" | custom-call | tf_op jit(solution)/shard_map/jit(cholesky)/cholesky | solution.py:62
  807.7 9.8 %custom-call.32 = f32[1,128,128]{1,2,0:T(8,128)S(1)} custom-call(f32[1,128,128]{2,1,0:T(8,128)S(1)} %get-tuple-element.38), custom_call_target="InvertDiagBlocksLowerTriangular" | custom-call | tf_op jit(solution)/shard_map/jit(cholesky)/cholesky | solution.py:62
  819.0 11.7 %cholesky.238 = f32[128,128]{1,0:T(8,128)S(1)} custom-call(f32[128,128]{1,0:T(8,128)S(1)} %cholesky.275), custom_call_target="Cholesky" | custom-call | tf_op jit(solution)/shard_map/jit(cholesky)/cholesky | solution.py:62
  831.5 9.8 %custom-call.33 = f32[1,128,128]{1,2,0:T(8,128)S(1)} custom-call(f32[1,128,128]{2,1,0:T(8,128)S(1)} %get-tuple-element.35), custom_call_target="InvertDiagBlocksLowerTriangular" | custom-call | tf_op jit(solution)/shard_map/jit(cholesky)/cholesky | solution.py:62
  843.1 11.7 %cholesky.255 = f32[128,128]{1,0:T(8,128)S(1)} custom-call(f32[128,128]{1,0:T(8,128)S(1)} %convolution_subtract_fusion.5), custom_call_target="Cholesky" | custom-call | tf_op jit(solution)/shard_map/jit(cholesky)/cholesky | solution.py:62
  859.3 14.1 %while.1 = (s32[]{:T(128)}, f32[512,512]{1,0:T(8,128)}, s32[4,2]{0,1:T(2,128)S(1)}, f32[4,128,128]{2,1,0:T(8,128)}, s32[]{:T(128)}) while((s32[]{:T(128)}, f32[512,512]{1,0:T(8,128)}, s32[4,2]{0,1:T(2,128)S(1)}, f32[4,128,128]{2,1,0:T(8,128)}, s32[]{:T(128)}) %tuple.37), condition=%wide.while_cond, body=%wide.while_body.sunk | while | flops 2 | bytes 132705 | solution.py:63
  860.0 2.9 bitcast_dynamic-update-slice_fusion.2
  863.5 2.9 bitcast_dynamic-update-slice_fusion.2
  867.0 2.9 bitcast_dynamic-update-slice_fusion.2
  870.6 2.8 bitcast_dynamic-update-slice_fusion.2
  873.4 40.1 %custom-call.34 = f32[4,128,128]{1,2,0:T(8,128)S(1)} custom-call(f32[4,128,128]{2,1,0:T(8,128)} %get-tuple-element.9), custom_call_target="InvertDiagBlocksLowerTriangular" | custom-call | tf_op jit(solution)/shard_map/jit(_solve_triangular)/triangular_solve | solution.py:63
  919.4 8.7 convolution_bitcast_fusion
  928.1 5.3 copy.29
  (82 shorter events, 38.5 us)
Async XLA Ops:
  23.5 12.6 %copy-start.4 = (s32[4,16384]{1,0:T(4,128)S(1)}, s32[4,16384]{1,0:T(4,128)}, u32[]{:S(2)}) copy-start(s32[4,16384]{1,0:T(4,128)} %param.5) | copy-start | bytes 786436
  23.5 13.1 %copy-start.5 = (s32[2]{0:T(128)S(1)}, s32[2]{0:T(128)}, u32[]{:S(2)}) copy-start(s32[2]{0:T(128)} %constant.238) | copy-start | bytes 28
  23.5 13.4 %copy-start.6 = (s32[2]{0:T(128)S(1)}, s32[2]{0:T(128)}, u32[]{:S(2)}) copy-start(s32[2]{0:T(128)} %constant.241) | copy-start | bytes 28
  23.5 253.5 %all-to-all-start = ((f32[4,512,512]{2,0,1:T(4,128)}), f32[4,512,512]{2,0,1:T(4,128)}, u32[]{:S(2)}, u32[]{:S(2)}) async-start(f32[4,512,512]{2,0,1:T(4,128)} %copy.18), calls=%async_computation | async-start | bytes 8388608 | tf_op jit(solution)/shard_map/all_to_all | solution.py:47
  36.0 731.0 %all-reduce.3.cloned.1.call-start = ((), (), s32[]{:S(2)}) async-start(), calls=%async_computation.2 | async-start | bytes 2097152 | tf_op jit(solution)/shard_map/psum | solution.py:60
  767.1 1.8 copy-start.1
  769.1 1.0 copy-start.3
  791.7 122.1 %copy-start.2 = (f32[512,512]{1,0:T(8,128)S(1)}, f32[512,512]{1,0:T(8,128)}, u32[]{:S(2)}) copy-start(f32[512,512]{1,0:T(8,128)} %fusion.23) | copy-start | bytes 3145732
  913.5 5.9 copy-start
Sparse Core Ops, SparseCore 0:
  511.9 255.1 all-reduce.2
where the time goes:
time: 951 us; the launch traced here: 942 us
  local copies, waits for them, and re-layouts  417 us (44%)
  waiting for transfers between devices  254 us (27%)
  other arithmetic  138 us (15%)
  blocking collectives  62 us (7%)
  matrix products  41.3 us (4%)
  between operations  17.2 us (2%)
  starting transfers between devices  12.6 us (1%)
    unnamed x22, local copies, waits for them, and re-layouts  330 us
    psum x1, waiting for transfers between devices, local(): gram = lax.psum(gram, ('rows', 'grp'))  254 us
    another operation x15, other arithmetic, local(): lower = jnp.linalg.cholesky(gram)  79.3 us
    all_to_all x1, blocking collectives, local(): lax.all_to_all(picked, 'rows', split_axis=2, concat_axis=1, tiled=True)  62 us
    another operation x3, other arithmetic, local(): jax.scipy.linalg.solve_triangular(lower, jnp.eye(width, dtype=jnp.float32...  41.4 us
    all_to_all x2, local copies, waits for them, and re-layouts, local(): lax.all_to_all(picked, 'rows', split_axis=2, concat_axis=1, tiled=True)  24.2 us
    select_n x1, local copies, waits for them, and re-layouts, local(): picked = jnp.where(parity[:, None, :] == 1, odd_rows, even_rows)  20.2 us
  transfers between devices with their start and end apart: 2, of which 1 were waited for; matrix products, arithmetic and copies ran while one was open for 26% of the time, Pallas kernels for 0%

commit v1 on v0

--- a/solution.py
+++ b/solution.py
@@ -2,8 +2,12 @@
 import jax.numpy as jnp
 from jax import lax
 from jax.sharding import PartitionSpec as P
+from jax.lax import all_to_all, psum
 
 INNER = 256
+note_zone_for = lambda frame: jnp.concatenate(
+    all_to_all(jnp.stack(jnp.split(frame, psum(1, "rows"), axis=2), axis=0), "rows", 0, 0), axis=1
+)
 
 
 def cosine_sorted(size):
@@ -55,7 +59,7 @@
     even_rows = mixed[:, :, :, :halfin].reshape(batches, narrow, half)
     odd_rows = mixed[:, :, :, halfin:].reshape(batches, narrow, half)
     picked = jnp.where(parity[:, None, :] == 1, odd_rows, even_rows)
-    rows_back = lax.all_to_all(picked, "rows", split_axis=2, concat_axis=1, tiled=True)
+    rows_back = note_zone_for(picked)
     gram = jnp.einsum("bnr,bmr->nm", rows_back, rows_back, precision=lax.Precision.HIGHEST)
     gram = lax.psum(gram, ("rows", "grp"))
     gram = gram / (ngroups * batches * half)

time: 951 us -> 803 us (0.84)
  local copies, waits for them, and re-layouts: 417 us -> 287 us
    unnamed x22 -> x81, local copies, waits for them, and re-layouts: 330 us -> 247 us
    all_to_all x2 -> x0, local copies, waits for them, and re-layouts: 24.2 us -> none  [local(): lax.all_to_all(picked, 'rows', split_axis=2, concat_axis=1, tiled=True)]
    select_n x1 -> x0, local copies, waits for them, and re-layouts: 20.2 us -> none  [local(): picked = jnp.where(parity[:, None, :] == 1, odd_rows, even_rows)]
  transfers between devices with their start and end apart: 2 -> 2, of which waited for: 1 -> 1; matrix products, arithmetic and copies ran while one was open for 26% -> 30% of each run, Pallas kernels for 0% -> 0%
where the time goes in v1:
time: 803 us; the launch traced here: 796 us
  local copies, waits for them, and re-layouts  287 us (36%)
  waiting for transfers between devices  254 us (32%)
  other arithmetic  129 us (16%)
  blocking collectives  61.4 us (8%)
  matrix products  34.5 us (4%)
  between operations  17.7 us (2%)
  starting transfers between devices  12.5 us (2%)
    psum x1, waiting for transfers between devices, local(): gram = lax.psum(gram, ('rows', 'grp'))  254 us
    unnamed x81, local copies, waits for them, and re-layouts  247 us
    another operation x15, other arithmetic, local(): lower = jnp.linalg.cholesky(gram)  79.6 us
    all_to_all x1, blocking collectives, all_to_all(jnp.stack(jnp.split(frame, psum(1, 'rows'), axis=2), axis=0),...  61.4 us
    another operation x3, other arithmetic, local(): jax.scipy.linalg.solve_triangular(lower, jnp.eye(width, dtype=jnp.float32...  40.4 us
  transfers between devices with their start and end apart: 2, of which 1 were waited for; matrix products, arithmetic and copies ran while one was open for 30% of the time, Pallas kernels for 0%

profile of v1, /device:TPU:2, one launch (start us, length us, event | category | flops | bytes accessed | tf_op | source)
XLA Modules:
  0.0 796.5 jit_solution(2821581498170756660)
XLA Ops:
  7.9 2.5 broadcast_multiply_fusion
  10.5 7.6 fusion.31
  18.0 5.4 copy.82
  23.5 12.5 %all-to-all-start = ((f32[4,512,512]{2,0,1:T(4,128)}), f32[4,512,512]{2,0,1:T(4,128)}, u32[]{:S(2)}, u32[]{:S(2)}) async-start(f32[4,512,512]{2,0,1:T(4,128)} %copy.82), calls=%async_computation | async-start | bytes 8388608 | tf_op jit(solution)/shard_map/all_to_all | solution.py:51
  37.3 239.7 %scatter_custom_fusion = s32[65536]{0:T(1024)S(1)} fusion(s32[65536]{0:T(1024)S(1)} %bitcast.360, s32[65536]{0:T(1024)S(1)} %bitcast.361, s32[]{:T(128)} %copy.187), kind=kCustom, calls=%fused_computation.148 | custom fusion | bytes 262148
  277.2 3.5 copy.107
  280.8 4.4 copy.84
  285.2 4.9 reshape.116
  290.1 8.8 %convolution_bitcast_fusion.1 = f32[4,8,128,256]{2,3,1,0:T(8,128)S(1)} fusion(f32[4,8,128,256]{3,2,1,0:T(8,128)} %reshape.116, s32[128]{0:T(128)S(1)} %get-tuple-element.45, f32[128]{0:T(128)S(1)} %fusion.88), kind=kOutput, calls=%fused_computation.5 | convolution fusion | flops 1610858496 | bytes 8389632 | tf_op jit(solution)/shard_map/ap,bcpq->bcaq/dot_general | solution.py:52
  300.6 1.9 copy.86
  302.5 1.7 reshape.117
  304.2 2.9 copy.87
  307.2 2.7 reshape.118
  309.9 1.9 broadcast_select_fusion
  312.6 61.4 %all_to_all.20 = f32[64,4,8,256]{3,2,1,0:T(8,128)S(1)} all-to-all(f32[64,4,8,256]{3,2,1,0:T(8,128)S(1)} %constant_dynamic-update-slice_fusion), channel_id=1, replica_groups=mesh['rows'=64,'grp'=4] {'rows'}, dimensions={0} | all-to-all | bytes 4194304 | tf_op jit(solution)/shard_map/all_to_all | solution.py:9
  373.9 4.5 fusion.3
  379.7 254.1 %all-reduce.3.cloned.1.call-done = f32[512,512]{0,1:T(8,128)} async-done(((f32[512,512]{0,1:T(8,128)}), f32[512,512]{0,1:T(8,128)}) %all-reduce.3.cloned.1.call-update) | async-done | bytes 1048592 | tf_op jit(solution)/shard_map/psum | solution.py:64
  635.8 11.7 %cholesky.104 = f32[128,128]{1,0:T(8,128)S(1)} custom-call(f32[128,128]{1,0:T(8,128)S(1)} %cholesky.266), custom_call_target="Cholesky" | custom-call | tf_op jit(solution)/shard_map/jit(cholesky)/cholesky | solution.py:66
  647.6 9.8 %custom-call.31 = f32[1,128,128]{1,2,0:T(8,128)S(1)} custom-call(f32[1,128,128]{2,1,0:T(8,128)S(1)} %get-tuple-element.41), custom_call_target="InvertDiagBlocksLowerTriangular" | custom-call | tf_op jit(solution)/shard_map/jit(cholesky)/cholesky | solution.py:66
  658.1 12.1 %cholesky.217 = f32[128,128]{1,0:T(8,128)S(1)} custom-call(f32[128,128]{1,0:T(8,128)S(1)} %cholesky.270), custom_call_target="Cholesky" | custom-call | tf_op jit(solution)/shard_map/jit(cholesky)/cholesky | solution.py:66
  670.3 9.8 %custom-call.32 = f32[1,128,128]{1,2,0:T(8,128)S(1)} custom-call(f32[1,128,128]{2,1,0:T(8,128)S(1)} %get-tuple-element.38), custom_call_target="InvertDiagBlocksLowerTriangular" | custom-call | tf_op jit(solution)/shard_map/jit(cholesky)/cholesky | solution.py:66
  680.8 11.7 %cholesky.238 = f32[128,128]{1,0:T(8,128)S(1)} custom-call(f32[128,128]{1,0:T(8,128)S(1)} %cholesky.275), custom_call_target="Cholesky" | custom-call | tf_op jit(solution)/shard_map/jit(cholesky)/cholesky | solution.py:66
  692.5 9.8 %custom-call.33 = f32[1,128,128]{1,2,0:T(8,128)S(1)} custom-call(f32[1,128,128]{2,1,0:T(8,128)S(1)} %get-tuple-element.35), custom_call_target="InvertDiagBlocksLowerTriangular" | custom-call | tf_op jit(solution)/shard_map/jit(cholesky)/cholesky | solution.py:66
  702.9 11.9 %cholesky.255 = f32[128,128]{1,0:T(8,128)S(1)} custom-call(f32[128,128]{1,0:T(8,128)S(1)} %convolution_subtract_fusion.5), custom_call_target="Cholesky" | custom-call | tf_op jit(solution)/shard_map/jit(cholesky)/cholesky | solution.py:66
  721.6 10.5 %while.1 = (s32[]{:T(128)}, f32[512,512]{1,0:T(8,128)S(1)}, s32[4,2]{0,1:T(2,128)S(1)}, f32[4,128,128]{2,1,0:T(8,128)}, s32[]{:T(128)}) while((s32[]{:T(128)}, f32[512,512]{1,0:T(8,128)S(1)}, s32[4,2]{0,1:T(2,128)S(1)}, f32[4,128,128]{2,1,0:T(8,128)}, s32[]{:T(128)}) %tuple.37), condition=%wide.while_cond, body=%wide.while_body.sunk | while | flops 2 | bytes 132205 | solution.py:67
  722.3 2.0 bitcast_dynamic-update-slice_fusion.2
  724.9 2.0 bitcast_dynamic-update-slice_fusion.2
  727.5 2.0 bitcast_dynamic-update-slice_fusion.2
  730.2 2.0 bitcast_dynamic-update-slice_fusion.2
  732.1 40.1 %custom-call.34 = f32[4,128,128]{1,2,0:T(8,128)S(1)} custom-call(f32[4,128,128]{2,1,0:T(8,128)} %get-tuple-element.9), custom_call_target="InvertDiagBlocksLowerTriangular" | custom-call | tf_op jit(solution)/shard_map/jit(_solve_triangular)/triangular_solve | solution.py:67
  775.4 8.7 %convolution_bitcast_fusion = f32[2048,512]{0,1:T(8,128)} fusion(f32[2048,512]{1,0:T(8,128)S(1)} %copy-done, f32[128,512]{1,0:T(8,128)S(1)} %fusion.65, f32[128,512]{1,0:T(8,128)S(1)} %fusion.66, f32[128,512]{1,0:T(8,128)S(1)} %fusion.68, f32[128,512]{1,0:T(8,128)S(1)} %fusion.37), kind=kOutput, calls=%fused_computation.4 | convolution fusion | flops 6443237376 | bytes 9437184 | tf_op jit(solution)/shard_map/dot_general | solution.py:70
  784.1 5.3 copy.92
  (138 shorter events, 19.3 us)
Async XLA Ops:
  23.5 12.6 %copy-start.3 = (s32[4,16384]{1,0:T(4,128)S(1)}, s32[4,16384]{1,0:T(4,128)}, u32[]{:S(2)}) copy-start(s32[4,16384]{1,0:T(4,128)} %param.5) | copy-start | bytes 786436
  23.5 13.1 %copy-start.4 = (s32[2]{0:T(128)S(1)}, s32[2]{0:T(128)}, u32[]{:S(2)}) copy-start(s32[2]{0:T(128)} %constant.238) | copy-start | bytes 28
  23.5 13.4 %copy-start.5 = (s32[2]{0:T(128)S(1)}, s32[2]{0:T(128)}, u32[]{:S(2)}) copy-start(s32[2]{0:T(128)} %constant.241) | copy-start | bytes 28
  23.5 253.7 %all-to-all-start = ((f32[4,512,512]{2,0,1:T(4,128)}), f32[4,512,512]{2,0,1:T(4,128)}, u32[]{:S(2)}, u32[]{:S(2)}) async-start(f32[4,512,512]{2,0,1:T(4,128)} %copy.82), calls=%async_computation | async-start | bytes 8388608 | tf_op jit(solution)/shard_map/all_to_all | solution.py:51
  36.0 597.7 %all-reduce.3.cloned.1.call-start = ((), (), s32[]{:S(2)}) async-start(), calls=%async_computation.2 | async-start | bytes 2097152 | tf_op jit(solution)/shard_map/psum | solution.py:64
  633.7 1.8 copy-start.1
  720.3 52.3 %copy-start.2 = (f32[512,512]{1,0:T(8,128)S(1)}, f32[512,512]{1,0:T(8,128)}, u32[]{:S(2)}) copy-start(f32[512,512]{1,0:T(8,128)} %fusion.24) | copy-start | bytes 3145732
  773.0 2.4 copy-start
Sparse Core Ops, SparseCore 0:
  378.6 255.0 all-reduce.2
